TPU v7x, 32 devices: a whole 2x2x4 slice. The times are simulated.
32 devices in a mesh: sub: 8 (over y, x, core), tm: 4 (over z).
Axes of the slice: x: 2, y: 2, z: 4, core: 2. Of those that a mesh axis runs over, the one named last changes fastest.
Arguments:
- voltages: bfloat16 [8192, 12, 2, 2048], P('sub', 'tm'), may hold values from -6 to 6
- slot_feed: int32 [2048], replicated, may hold values from 0 to 2047, each once
- chan_lag: int32 [8192], replicated, may hold values from 0 to 4096
- trial_dm: int32 [512], replicated, may hold values from 0 to 4096
- beam_order: int32 [1024], replicated, may hold values from 0 to 1023, each once
Outputs:
- dedispersed: float32 [1024, 12, 512], P('sub', 'tm')
Inputs may be any that keep to these rules, and one draw needn't show every extreme that they name: `slot_feed`: each feed once; slot (p * 4 + y) * 256 + n is polarization p at east-west position y and north-south position n. `beam_order`: each beam once.
All inputs are finite; a program needn't handle non-finite values.
Results may differ from a plain program's by a relative error of at most 0.00088.
Values may be sent and summed in bfloat16 or wider, within the bound.
No kernel may reach another device: no remote copies, remote signals or barrier semaphores. Data moves between devices by JAX's collectives and lax.ppermute only.
A program may use at most 192 MiB of HBM per device.

v0:
```python
import math
import jax
import jax.numpy as jnp
from jax import lax
from jax.sharding import PartitionSpec as P

NS = 256
CYL = 4
POL = 2
CHANNELS = 8192
NDM = 512
MAXD = 6
QUANT = 2796202


def shifted(value, axis, steps):
    count = lax.axis_size(axis)
    initial, last = (max(0, -steps), min(count, count - steps))
    return lax.ppermute(value, axis, [(source, source + steps) for source in range(initial, last)])


def north_table():
    positions = jnp.arange(NS, dtype=jnp.int32)
    phase_index = positions[:, None] * positions[None, :] % NS
    angles = phase_index.astype(jnp.float32) * (2.0 * math.pi / NS)
    cosine = jnp.cos(angles) / math.sqrt(NS)
    sine_part = jnp.sin(angles) / math.sqrt(NS)
    real_row = jnp.stack([cosine, -sine_part], axis=1)
    imag_row = jnp.stack([sine_part, cosine], axis=1)
    return jnp.stack([real_row, imag_row], axis=0).astype(jnp.bfloat16)


def west_table():
    cylinder = jnp.arange(CYL, dtype=jnp.int32)
    quarter_turn = cylinder[:, None] * cylinder[None, :] % 4
    cosine = (quarter_turn == 0).astype(jnp.float32) - (quarter_turn == 2).astype(jnp.float32)
    sine_part = (quarter_turn == 1).astype(jnp.float32) - (quarter_turn == 3).astype(jnp.float32)
    real_row = jnp.stack([cosine, -sine_part], axis=2)
    imag_row = jnp.stack([sine_part, cosine], axis=2)
    return 0.5 * jnp.stack([real_row, imag_row], axis=1)


def compute_power(north_beams):
    west_beams = jnp.einsum(
        "ctpyom,yoeq->ctpeqm", north_beams, west_table(), precision=lax.Precision.HIGHEST
    )
    squares = jnp.sum(west_beams * west_beams, axis=(2, 4))
    return squares.reshape(north_beams.shape[0], north_beams.shape[1], CYL * NS)


def delay_table(lag_rows, trial_dm):
    return lag_rows[:, None] * trial_dm[None, :] // QUANT


def shift_sum(source, delays, head_rows, out_rows):
    time_rows = source.shape[1]
    total_sum = jnp.zeros((source.shape[2], out_rows, NDM), jnp.float32)
    for delay_step in range(MAXD + 1):
        onehot = (delays == delay_step).astype(jnp.bfloat16)
        first_index = head_rows - delay_step
        begin_row = max(0, first_index)
        end_row = min(time_rows, first_index + out_rows)
        part = jnp.einsum("ctb,cd->btd", source, onehot, preferred_element_type=jnp.float32)
        front_pad = begin_row - first_index
        back_pad = out_rows - front_pad - (end_row - begin_row)
        total_sum = total_sum + jnp.pad(part, ((0, 0), (front_pad, back_pad), (0, 0)))
    return total_sum


def per_device(voltages, slot_feed, chan_lag, trial_dm, beam_order):
    channel_count = voltages.shape[0]
    sample_count = voltages.shape[1]
    shard_reach = (MAXD + sample_count - 1) // sample_count
    grid_volts = jnp.take(voltages, slot_feed, axis=3).reshape(
        channel_count, sample_count, 2, POL, CYL, NS
    )
    north_beams = jnp.einsum(
        "ctrpyn,rnom->ctpyom", grid_volts, north_table(), preferred_element_type=jnp.float32
    )
    intensity = compute_power(north_beams)
    ordered = jnp.take(intensity, beam_order, axis=2)
    totals = lax.psum(jnp.sum(ordered, axis=1), "tm")
    average = totals / (sample_count * lax.axis_size("tm"))
    normal = (ordered - average[:, None, :]).astype(jnp.bfloat16)
    head_rows = 0
    out_rows = sample_count + MAXD
    offset = lax.axis_index("sub") * channel_count
    lag_rows = lax.dynamic_slice_in_dim(chan_lag, offset, channel_count)
    delays = delay_table(lag_rows, trial_dm)
    result = lax.psum_scatter(
        shift_sum(normal, delays, head_rows, out_rows), "sub", scatter_dimension=0, tiled=True
    )
    kept_rows = result[:, :sample_count, :]
    for distance in range(1, shard_reach + 1):
        first_row = distance * sample_count
        last_row = min(first_row + sample_count, sample_count + MAXD)
        carried = shifted(result[:, first_row:last_row, :], "tm", distance)
        kept_rows = kept_rows + carried
    result = kept_rows
    return result / math.sqrt(CHANNELS)


def solution(mesh):
    return jax.shard_map(
        per_device,
        mesh=mesh,
        in_specs=(P("sub", "tm", None, None), P(), P(), P(), P()),
        out_specs=P("sub", "tm", None),
        check_vma=False,
    )
```

profile of v0, /device:TPU:24, one launch (start us, length us, event | category | flops | bytes accessed | tf_op | source)
XLA Modules:
  0.0 946.9 jit_solution(5524718804236857798)
XLA Ops:
  6.5 0.0 all-reduce.9.cloned.1.call-start
  6.5 1.1 negate_convert_fusion
  7.6 1.0 fusion.49
  8.6 0.7 fusion.54
  9.3 0.7 compare_and_fusion
  10.1 0.7 fusion.56
  10.8 0.7 compare_and_fusion.1
  11.5 84.4 %copy.39 = bf16[1024,3,2,2048]{0,1,2,3:T(4,128)(2,1)} copy(bf16[1024,3,2,2048]{3,2,1,0:T(2,128)(2,1)} %param.5) | data formatting | bytes 50331648 | tf_op args[0]
  95.8 71.0 %gather_fusion = bf16[2048,1024,3,2]{1,2,3,0:T(4,128)(2,1)} fusion(bf16[1024,3,2,2048]{0,1,2,3:T(4,128)(2,1)} %copy.39, s32[2048]{0:T(1024)S(1)} %fusion.54), kind=kCustom, calls=%fused_computation | custom fusion | bytes 50339840 | tf_op jit(solution)/shard_map/jit(_take)/gather | solution.py:74
  166.9 48.4 %copy.40 = bf16[1024,3,2,2,4,256]{5,0,2,4,3,1:T(8,128)(2,1)} copy(bf16[1024,3,2,2,4,256]{0,1,2,5,4,3:T(4,128)(2,1)} %bitcast.98) | data formatting | bytes 50331648 | tf_op jit(solution)/shard_map/jit(_take)/gather | solution.py:74
  215.3 0.1 copy.37
  215.4 0.1 copy.38
  215.6 27.5 %fusion.8 = f32[1024,3,2,4,2,256]{5,0,4,3,2,1:T(8,128)} fusion(bf16[1024,3,2,2,4,256]{5,0,2,4,3,1:T(8,128)(2,1)} %copy.40, pred[2,4,256]{2,1,0:T(4,128)(4,1)S(1)} %broadcast_in_dim.34, bf16[1,256,2,256]{3,1,0,2:T(8,128)(2,1)S(1)} %get-tuple-element.8, bf16[1,256,2,256]{3,1,0,2:T(8,128)(2,1)S(1)} %get-tuple-element.7), kind=kOutput, calls=%fused_computation.11 | convolution fusion | flops 12898533376 | bytes 76023808 | tf_op jit(solution)/shard_map/ctrpyn,rnom->ctpyom/dot_general | solution.py:77
  243.0 186.1 %fusion = f32[4,1024,3,256]{3,0,2,1:T(4,128)} fusion(f32[1024,3,2,4,2,256]{5,0,4,3,2,1:T(8,128)} %fusion.8, f32[4,2,4,2,1,1,1]{0,2,1,6,5,4,3:T(4,128)S(1)} %fusion.107), kind=kOutput, calls=%fused_computation.3 | convolution fusion | flops 1229979648 | bytes 62914816 | tf_op jit(solution)/shard_map/ctpyom,yoeq->ctpeqm/dot_general | solution.py:44
  429.2 14.6 %copy.43 = f32[1024,3,4,256]{0,3,2,1:T(8,128)} copy(f32[1024,3,4,256]{3,2,1,0:T(4,128)} %bitcast.100) | data formatting | bytes 25165824 | tf_op jit(solution)/shard_map/reduce_sum | solution.py:47
  443.8 18.1 %copy.44 = f32[1024,3,1024]{0,1,2:T(4,128)} copy(f32[1024,3,1024]{0,2,1:T(8,128)} %bitcast.99) | data formatting | bytes 25165824 | tf_op jit(solution)/shard_map/reshape | solution.py:48
  461.8 26.0 %gather_fusion.1 = f32[1024,1024,3]{1,2,0:T(4,128)} fusion(f32[1024,3,1024]{0,1,2:T(4,128)} %copy.44, s32[1024]{0:T(1024)S(1)} %fusion.56), kind=kCustom, calls=%fused_computation.1 | custom fusion | bytes 25169920 | tf_op jit(solution)/shard_map/jit(_take)/gather | solution.py:81
  487.8 17.4 %copy.45 = f32[1024,1024,3]{0,1,2:T(8,128)} copy(f32[1024,1024,3]{1,2,0:T(4,128)} %gather_fusion.1) | data formatting | bytes 25165824 | tf_op jit(solution)/shard_map/jit(_take)/gather | solution.py:81
  505.2 8.8 bitcast_reduce_fusion
  514.0 0.0 all-reduce.9.cloned.1.call-update
  514.0 0.3 reduce-scatter.2.cloned.1.call-start
  514.3 0.7 dynamic_slice.3
  514.9 152.9 %all-reduce.9.cloned.1.call-done = f32[1024,1024]{1,0:T(8,128)} async-done(((f32[1024,1024]{1,0:T(8,128)}), f32[1024,1024]{1,0:T(8,128)}) %all-reduce.9.cloned.1.call-update) | async-done | bytes 4194320 | tf_op jit(solution)/shard_map/psum | solution.py:82
  667.8 5.1 broadcast_multiply_fusion
  673.0 0.0 copy-start.1
  673.0 10.9 %fusion.11 = bf16[1024,3,1024]{2,0,1:T(8,128)(2,1)} fusion(f32[1024,1024,3]{0,1,2:T(8,128)} %copy.45, f32[1024,1024]{1,0:T(8,128)} %broadcast_multiply_fusion, pred[1024]{0:T(1024)(128)(4,1)S(1)} %compare_and_fusion.1), kind=kLoop, calls=%fused_computation.15 | loop fusion | flops 9437184 | bytes 23069696 | tf_op jit(solution)/shard_map/convert_element_type | solution.py:84
  683.9 0.0 copy-done.1
  683.9 0.0 copy-start
  683.9 7.8 convolution_bitcast_fusion.1
  691.7 0.0 copy-done
  691.7 5.3 convolution_bitcast_fusion.2
  697.0 7.2 convolution_bitcast_fusion.3
  704.1 7.3 convolution_bitcast_fusion.4
  711.4 7.2 convolution_bitcast_fusion.5
  718.6 7.1 convolution_bitcast_fusion.6
  725.8 7.6 convolution_bitcast_fusion
  733.3 20.4 %pad_add_fusion = f32[1024,9,512]{0,2,1:T(8,128)} fusion(f32[1024,3,512]{0,2,1:T(8,128)} %convolution_bitcast_fusion, f32[1024,3,512]{0,2,1:T(8,128)S(1)} %convolution_bitcast_fusion.1, f32[1024,3,512]{0,2,1:T(8,128)S(1)} %convolution_bitcast_fusion.2, f32[1024,3,512]{0,2,1:T(8,128)} %convolution_bitcast_fusion.3, ...), kind=kLoop, calls=%fused_computation.12 | loop fusion | flops 28311552 | bytes 62914560 | tf_op jit(solution)/shard_map/add | solution.py:66
  753.8 0.0 reduce-scatter.2.cloned.1.call-update
  753.8 127.6 %reduce-scatter.2.cloned.1.call-done = f32[128,9,512]{0,2,1:T(8,128)} async-done(((f32[1024,9,512]{0,2,1:T(8,128)}), f32[128,9,512]{0,2,1:T(8,128)}) %reduce-scatter.2.cloned.1.call-update) | async-done | bytes 2359312 | tf_op jit(solution)/shard_map/reduce_scatter | solution.py:90
  881.4 1.5 fusion.96
  882.8 1.3 collective-permute-start
  884.1 1.3 collective-permute-start.1
  885.4 18.8 %collective-permute-done = f32[128,3,512]{0,2,1:T(8,128)S(1)} collective-permute-done((f32[128,3,512]{0,2,1:T(8,128)S(1)}, f32[128,3,512]{0,2,1:T(8,128)S(1)}, u32[]{:S(2)}, u32[]{:S(2)}) %collective-permute-start) | collective-permute-done | bytes 786464 | tf_op jit(solution)/shard_map/ppermute | solution.py:19
  904.3 33.3 %collective-permute-done.1 = f32[128,3,512]{0,2,1:T(8,128)S(1)} collective-permute-done((f32[128,3,512]{0,2,1:T(8,128)S(1)}, f32[128,3,512]{0,2,1:T(8,128)S(1)}, u32[]{:S(2)}, u32[]{:S(2)}) %collective-permute-start.1) | collective-permute-done | bytes 786464 | tf_op jit(solution)/shard_map/ppermute | solution.py:19
  937.5 1.2 fusion.40
  938.8 1.1 copy.46
  (6 shorter events, 0.1 us)
Async XLA Ops:
  6.5 661.3 %all-reduce.9.cloned.1.call-start = ((), (), s32[]{:S(2)}) async-start(), calls=%async_computation.1 | async-start | bytes 8388608 | tf_op jit(solution)/shard_map/psum | solution.py:82
  514.0 367.4 %reduce-scatter.2.cloned.1.call-start = ((), (), s32[]{:S(2)}) async-start(), calls=%async_computation.2 | async-start | bytes 21233664 | tf_op jit(solution)/shard_map/reduce_scatter | solution.py:90
  673.0 10.9 %copy-start.1 = (s32[512]{0:T(512)S(1)}, s32[512]{0:T(512)}, u32[]{:S(2)}) copy-start(s32[512]{0:T(512)} %param.8) | copy-start | bytes 6148
  683.9 7.8 copy-start
  882.8 21.4 %collective-permute-start = (f32[128,3,512]{0,2,1:T(8,128)S(1)}, f32[128,3,512]{0,2,1:T(8,128)S(1)}, u32[]{:S(2)}, u32[]{:S(2)}) collective-permute-start(f32[128,3,512]{0,2,1:T(8,128)S(1)} %get-tuple-element.5), channel_id=1, source_target_pairs={{0,1},{1,2},{2,3},{4,5},{5,6},{6,7},{8,9},{9,10},{10,11},{12,13},{... | collective-permute-start | bytes 2359304 | tf_op jit(solution)/shard_map/ppermute | solution.py:19
  884.1 53.4 %collective-permute-start.1 = (f32[128,3,512]{0,2,1:T(8,128)S(1)}, f32[128,3,512]{0,2,1:T(8,128)S(1)}, u32[]{:S(2)}, u32[]{:S(2)}) collective-permute-start(f32[128,3,512]{0,2,1:T(8,128)S(1)} %get-tuple-element.6), channel_id=1, source_target_pairs={{0,2},{1,3},{4,6},{5,7},{8,10},{9,11},{12,14},{13,15},{16,18},{17,... | collective-permute-start | bytes 2359304 | tf_op jit(solution)/shard_map/ppermute | solution.py:19
Sparse Core Ops, SparseCore 0:
  514.1 153.6 all-reduce.8
  753.9 127.4 reduce-scatter.1
where the time goes:
time: 961 us; the launch traced here: 947 us
  waiting for transfers between devices  333 us (35%)
  local copies, waits for them, and re-layouts  283 us (29%)
  matrix products  263 us (27%)
  other arithmetic  51.4 us (5%)
  between operations  13.6 us (1%)
    dot_general x1, matrix products, compute_power(): jnp.einsum('ctpyom,yoeq->ctpeqm', north_beams, west_table(), precision=la...  186 us
    psum x1, waiting for transfers between devices, per_device(): totals = lax.psum(jnp.sum(ordered, axis=1), 'tm')  153 us
    reduce_scatter x1, waiting for transfers between devices, per_device(): lax.psum_scatter(shift_sum(normal, delays, head_rows, out_rows), 'sub', s...  128 us
    gather x2, local copies, waits for them, and re-layouts, per_device(): jnp.take(voltages, slot_feed, axis=3)  119 us
    unnamed x5, local copies, waits for them, and re-layouts  84.4 us
    ppermute x2, waiting for transfers between devices, shifted(): lax.ppermute(value, axis, [(source, source + steps) for source in range(i...  52.1 us
    dot_general x7, matrix products, shift_sum(): jnp.einsum('ctb,cd->btd', source, onehot, preferred_element_type=jnp.floa...  49.5 us
    gather x2, local copies, waits for them, and re-layouts, per_device(): ordered = jnp.take(intensity, beam_order, axis=2)  43.4 us
  transfers between devices with their start and end apart: 4, of which 4 were waited for; matrix products, arithmetic and copies ran while one was open for 0% of the time, Pallas kernels for 0%

commit v1 on v0

--- a/solution.py
+++ b/solution.py
@@ -79,7 +79,7 @@
     )
     intensity = compute_power(north_beams)
     ordered = jnp.take(intensity, beam_order, axis=2)
-    totals = lax.psum(jnp.sum(ordered, axis=1), "tm")
+    totals = jnp.sum(lax.all_gather(jnp.sum(ordered, axis=1), "tm"), axis=0)
     average = totals / (sample_count * lax.axis_size("tm"))
     normal = (ordered - average[:, None, :]).astype(jnp.bfloat16)
     head_rows = 0

time: 961 us -> 1140 us (1.19)
  waiting for transfers between devices: 333 us -> 464 us
  local copies, waits for them, and re-layouts: 283 us -> 315 us
  other arithmetic: 51.4 us -> 66.1 us
    all_gather x0 -> x1, waiting for transfers between devices: none -> 284 us  [per_device(): totals = jnp.sum(lax.all_gather(jnp.sum(ordered, axis=1), 'tm'), axis=0)]
    psum x1 -> x0, waiting for transfers between devices: 153 us -> none  [per_device(): totals = lax.psum(jnp.sum(ordered, axis=1), 'tm')]
    all_gather x0 -> x1, local copies, waits for them, and re-layouts: none -> 20.4 us  [per_device(): totals = jnp.sum(lax.all_gather(jnp.sum(ordered, axis=1), 'tm'), axis=0)]
    reduce_sum x1 -> x2, other arithmetic: 8.76 us -> 23.5 us  [per_device(): totals = jnp.sum(lax.all_gather(jnp.sum(ordered, axis=1), 'tm'), axis=0)]
    unnamed x5 -> x6, local copies, waits for them, and re-layouts: 84.4 us -> 89.7 us
where the time goes in v1:
time: 1140 us; the launch traced here: 1120 us
  waiting for transfers between devices  464 us (41%)
  local copies, waits for them, and re-layouts  315 us (28%)
  matrix products  263 us (23%)
  other arithmetic  66.1 us (6%)
  between operations  13.7 us (1%)
    all_gather x1, waiting for transfers between devices, per_device(): totals = jnp.sum(lax.all_gather(jnp.sum(ordered, axis=1), 'tm'), axis=0)  284 us
    dot_general x1, matrix products, compute_power(): jnp.einsum('ctpyom,yoeq->ctpeqm', north_beams, west_table(), precision=la...  186 us
    reduce_scatter x1, waiting for transfers between devices, per_device(): lax.psum_scatter(shift_sum(normal, delays, head_rows, out_rows), 'sub', s...  128 us
    gather x2, local copies, waits for them, and re-layouts, per_device(): jnp.take(voltages, slot_feed, axis=3)  119 us
    unnamed x6, local copies, waits for them, and re-layouts  89.7 us
    ppermute x2, waiting for transfers between devices, shifted(): lax.ppermute(value, axis, [(source, source + steps) for source in range(i...  52.1 us
    dot_general x7, matrix products, shift_sum(): jnp.einsum('ctb,cd->btd', source, onehot, preferred_element_type=jnp.floa...  49.3 us
    gather x2, local copies, waits for them, and re-layouts, per_device(): ordered = jnp.take(intensity, beam_order, axis=2)  43.4 us
  transfers between devices with their start and end apart: 4, of which 4 were waited for; matrix products, arithmetic and copies ran while one was open for 0% of the time, Pallas kernels for 0%

profile of v1, /device:TPU:24, one launch (start us, length us, event | category | flops | bytes accessed | tf_op | source)
XLA Modules:
  0.0 1123.9 jit_solution(18429372571359393546)
XLA Ops:
  6.5 0.0 all-gather.3.cloned.1.call-start
  6.5 1.1 negate_convert_fusion
  7.6 1.0 fusion.49
  8.6 0.7 fusion.54
  9.3 0.7 compare_and_fusion
  10.1 0.7 fusion.56
  10.8 0.7 compare_and_fusion.1
  11.5 84.4 %copy.50 = bf16[1024,3,2,2048]{0,1,2,3:T(4,128)(2,1)} copy(bf16[1024,3,2,2048]{3,2,1,0:T(2,128)(2,1)} %param.5) | data formatting | bytes 50331648 | tf_op args[0]
  95.8 71.0 %gather_fusion = bf16[2048,1024,3,2]{1,2,3,0:T(4,128)(2,1)} fusion(bf16[1024,3,2,2048]{0,1,2,3:T(4,128)(2,1)} %copy.50, s32[2048]{0:T(1024)S(1)} %fusion.54), kind=kCustom, calls=%fused_computation | custom fusion | bytes 50339840 | tf_op jit(solution)/shard_map/jit(_take)/gather | solution.py:74
  166.9 48.4 %copy.51 = bf16[1024,3,2,2,4,256]{5,0,2,4,3,1:T(8,128)(2,1)} copy(bf16[1024,3,2,2,4,256]{0,1,2,5,4,3:T(4,128)(2,1)} %bitcast.100) | data formatting | bytes 50331648 | tf_op jit(solution)/shard_map/jit(_take)/gather | solution.py:74
  215.3 0.1 copy.48
  215.4 0.1 copy.49
  215.6 27.5 %fusion.8 = f32[1024,3,2,4,2,256]{5,0,4,3,2,1:T(8,128)} fusion(bf16[1024,3,2,2,4,256]{5,0,2,4,3,1:T(8,128)(2,1)} %copy.51, pred[2,4,256]{2,1,0:T(4,128)(4,1)S(1)} %broadcast_in_dim.34, bf16[1,256,2,256]{3,1,0,2:T(8,128)(2,1)S(1)} %get-tuple-element.8, bf16[1,256,2,256]{3,1,0,2:T(8,128)(2,1)S(1)} %get-tuple-element.7), kind=kOutput, calls=%fused_computation.11 | convolution fusion | flops 12898533376 | bytes 76023808 | tf_op jit(solution)/shard_map/ctrpyn,rnom->ctpyom/dot_general | solution.py:77
  243.0 186.2 %fusion = f32[4,1024,3,256]{3,0,2,1:T(4,128)} fusion(f32[1024,3,2,4,2,256]{5,0,4,3,2,1:T(8,128)} %fusion.8, f32[4,2,4,2,1,1,1]{0,2,1,6,5,4,3:T(4,128)S(1)} %fusion.107), kind=kOutput, calls=%fused_computation.3 | convolution fusion | flops 1229979648 | bytes 62914816 | tf_op jit(solution)/shard_map/ctpyom,yoeq->ctpeqm/dot_general | solution.py:44
  429.2 14.6 %copy.54 = f32[1024,3,4,256]{0,3,2,1:T(8,128)} copy(f32[1024,3,4,256]{3,2,1,0:T(4,128)} %bitcast.102) | data formatting | bytes 25165824 | tf_op jit(solution)/shard_map/reduce_sum | solution.py:47
  443.8 18.1 %copy.55 = f32[1024,3,1024]{0,1,2:T(4,128)} copy(f32[1024,3,1024]{0,2,1:T(8,128)} %bitcast.101) | data formatting | bytes 25165824 | tf_op jit(solution)/shard_map/reshape | solution.py:48
  461.9 26.0 %gather_fusion.1 = f32[1024,1024,3]{1,2,0:T(4,128)} fusion(f32[1024,3,1024]{0,1,2:T(4,128)} %copy.55, s32[1024]{0:T(1024)S(1)} %fusion.56), kind=kCustom, calls=%fused_computation.1 | custom fusion | bytes 25169920 | tf_op jit(solution)/shard_map/jit(_take)/gather | solution.py:81
  487.9 17.4 %copy.56 = f32[1024,1024,3]{0,1,2:T(8,128)} copy(f32[1024,1024,3]{1,2,0:T(4,128)} %gather_fusion.1) | data formatting | bytes 25165824 | tf_op jit(solution)/shard_map/jit(_take)/gather | solution.py:81
  505.3 8.8 bitcast_reduce_fusion
  514.1 5.4 copy.65
  519.4 0.0 all-gather.3.cloned.1.call-update
  519.4 0.0 reduce-scatter.2.cloned.1.call-start
  519.5 0.7 dynamic_slice.3
  520.2 284.1 %all-gather.3.cloned.1.call-done = f32[4096,1024]{0,1:T(8,128)} async-done(((f32[1024,1024]{0,1:T(8,128)}), f32[4096,1024]{0,1:T(8,128)}) %all-gather.3.cloned.1.call-update) | async-done | bytes 16777232 | tf_op jit(solution)/shard_map/all_gather | solution.py:82
  804.3 20.4 %reshape.216 = f32[4,1024,1024]{1,0,2:T(4,128)} reshape(f32[4096,1024]{0,1:T(8,128)} %all-gather.3.cloned.1.call-done) | data formatting | bytes 33554432 | tf_op jit(solution)/shard_map/all_gather | solution.py:82
  824.7 14.7 %reduce_sum.32 = f32[1024,1024]{0,1:T(8,128)} reduce(f32[4,1024,1024]{1,0,2:T(4,128)} %reshape.216, f32[]{:T(128)} %constant.104.clone.1), dimensions={0}, to_apply=%region_2.3 | reduce | flops 3145728 | bytes 20971524 | tf_op jit(solution)/shard_map/reduce_sum | solution.py:82
  839.4 5.1 broadcast_multiply_fusion
  844.5 5.5 copy.58
  850.0 0.0 copy-start.1
  850.0 10.9 fusion.11
  861.0 0.0 copy-done.1
  861.0 7.8 convolution_bitcast_fusion.1
  868.8 5.0 convolution_bitcast_fusion.2
  873.8 7.6 convolution_bitcast_fusion.3
  881.4 7.3 convolution_bitcast_fusion.4
  888.7 7.2 convolution_bitcast_fusion.5
  895.9 7.1 convolution_bitcast_fusion.6
  903.0 7.3 convolution_bitcast_fusion
  910.3 20.4 %pad_add_fusion = f32[1024,9,512]{0,2,1:T(8,128)} fusion(f32[1024,3,512]{0,2,1:T(8,128)} %convolution_bitcast_fusion, f32[1024,3,512]{0,2,1:T(8,128)S(1)} %convolution_bitcast_fusion.1, f32[1024,3,512]{0,2,1:T(8,128)S(1)} %convolution_bitcast_fusion.2, f32[1024,3,512]{0,2,1:T(8,128)} %convolution_bitcast_fusion.3, ...), kind=kLoop, calls=%fused_computation.12 | loop fusion | flops 28311552 | bytes 62914560 | tf_op jit(solution)/shard_map/add | solution.py:66
  930.7 0.0 reduce-scatter.2.cloned.1.call-update
  930.7 127.6 %reduce-scatter.2.cloned.1.call-done = f32[128,9,512]{0,2,1:T(8,128)} async-done(((f32[1024,9,512]{0,2,1:T(8,128)}), f32[128,9,512]{0,2,1:T(8,128)}) %reduce-scatter.2.cloned.1.call-update) | async-done | bytes 2359312 | tf_op jit(solution)/shard_map/reduce_scatter | solution.py:90
  1058.3 1.5 fusion.96
  1059.8 1.3 collective-permute-start
  1061.1 1.3 collective-permute-start.1
  1062.4 18.8 %collective-permute-done = f32[128,3,512]{0,2,1:T(8,128)S(1)} collective-permute-done((f32[128,3,512]{0,2,1:T(8,128)S(1)}, f32[128,3,512]{0,2,1:T(8,128)S(1)}, u32[]{:S(2)}, u32[]{:S(2)}) %collective-permute-start) | collective-permute-done | bytes 786464 | tf_op jit(solution)/shard_map/ppermute | solution.py:19
  1081.2 33.3 %collective-permute-done.1 = f32[128,3,512]{0,2,1:T(8,128)S(1)} collective-permute-done((f32[128,3,512]{0,2,1:T(8,128)S(1)}, f32[128,3,512]{0,2,1:T(8,128)S(1)}, u32[]{:S(2)}, u32[]{:S(2)}) %collective-permute-start.1) | collective-permute-done | bytes 786464 | tf_op jit(solution)/shard_map/ppermute | solution.py:19
  1114.5 1.2 fusion.40
  1115.7 1.1 copy.59
  (8 shorter events, 0.1 us)
Async XLA Ops:
  6.5 797.7 %all-gather.3.cloned.1.call-start = ((), (), s32[]{:S(2)}) async-start(), calls=%async_computation.2 | async-start | bytes 20971520 | tf_op jit(solution)/shard_map/all_gather | solution.py:82
  519.4 538.9 %reduce-scatter.2.cloned.1.call-start = ((), (), s32[]{:S(2)}) async-start(), calls=%async_computation.1 | async-start | bytes 21233664 | tf_op jit(solution)/shard_map/reduce_scatter | solution.py:90
  850.0 11.0 copy-start.1
  861.0 7.8 copy-start
  1059.8 21.4 %collective-permute-start = (f32[128,3,512]{0,2,1:T(8,128)S(1)}, f32[128,3,512]{0,2,1:T(8,128)S(1)}, u32[]{:S(2)}, u32[]{:S(2)}) collective-permute-start(f32[128,3,512]{0,2,1:T(8,128)S(1)} %get-tuple-element.5), channel_id=1, source_target_pairs={{0,1},{1,2},{2,3},{4,5},{5,6},{6,7},{8,9},{9,10},{10,11},{12,13},{... | collective-permute-start | bytes 2359304 | tf_op jit(solution)/shard_map/ppermute | solution.py:19
  1061.1 53.4 %collective-permute-start.1 = (f32[128,3,512]{0,2,1:T(8,128)S(1)}, f32[128,3,512]{0,2,1:T(8,128)S(1)}, u32[]{:S(2)}, u32[]{:S(2)}) collective-permute-start(f32[128,3,512]{0,2,1:T(8,128)S(1)} %get-tuple-element.6), channel_id=1, source_target_pairs={{0,2},{1,3},{4,6},{5,7},{8,10},{9,11},{12,14},{13,15},{16,18},{17,... | collective-permute-start | bytes 2359304 | tf_op jit(solution)/shard_map/ppermute | solution.py:19
Sparse Core Ops, SparseCore 0:
  519.6 284.6 all-gather.2
  930.8 127.4 reduce-scatter.1
